TPU v7x, 512 devices: a whole 4x8x8 slice. The times are simulated.
512 devices in a mesh: cuts: 8 (over y), row: 64 (over x, z, core).
Axes of the slice: x: 4, y: 8, z: 8, core: 2. Of those that a mesh axis runs over, the one named last changes fastest.
Arguments:
- block_tiles: float32 [192, 24, 128, 128], P('row'), may hold values from -0.109375 to 0.109375
- tile_pattern: int32 [192, 24], P('row'), may hold values from 0 to 191, as said below
- start_vectors: float32 [8, 32, 24576], P('cuts', None, 'row'), may hold values from -8 to 8
- centers: float32 [8], P('cuts'), may hold values from -0.3 to 0.3
- halfwidths: float32 [8], P('cuts'), may hold values from 0.9 to 1.3
- dup_pairs: int32 [8, 8, 2], P('cuts'), may hold values from 0 to 31, as said below
Outputs:
- filtered_basis: float32 [8, 32, 24576], P('cuts', None, 'row')
- projected: float32 [8, 32, 32], P('cuts')
Inputs may be any that keep to these rules, and one draw needn't show every extreme that they name: tile_pattern[r, 0] = r; the other entries of block row r are distinct block rows, each within 12 of r cyclically and different from r. `dup_pairs`: within one slice the first entries of the pairs are distinct, and so are the second entries; the pairs of slice 0 are not used.
All inputs are finite; a program needn't handle non-finite values.
Results may differ from a plain program's by a relative error of at most 0.00015.
Values sent between devices are 32-bit elements; how exact they have to be, the bound alone decides.
A program may use at most 64 MiB of HBM per device.

v0:
```python
import math

import jax
import jax.numpy as jnp
from jax import lax
from jax.sharding import PartitionSpec as P

DEG = 8
REACH = 12


def from_behind(shard, axis, by):
    size = lax.axis_size(axis)
    return lax.ppermute(shard, axis, [(i, (i + by) % size) for i in range(size)])


def from_behind_2(value, axis, steps):
    count = lax.axis_size(axis)
    leading, last = (max(0, -steps), min(count, count - steps))
    return lax.ppermute(value, axis, [(source, source + steps) for source in range(leading, last)])


def apply_local(vectors, block_tiles, tile_pattern):
    vec_count = vectors.shape[0]
    local_rows = block_tiles.shape[0]
    tile_width = block_tiles.shape[2]
    device_reach = (REACH + local_rows - 1) // local_rows
    pieces = []
    for offset in range(-device_reach, device_reach + 1):
        if offset == 0:
            pieces.append(vectors)
        else:
            pieces.append(from_behind(vectors, "row", -offset))
    extended = jnp.concatenate(pieces, axis=1).reshape(
        vec_count, len(pieces) * local_rows, tile_width
    )
    total_rows = local_rows * lax.axis_size("row")
    lowest = (lax.axis_index("row") - device_reach) * local_rows
    positions = (tile_pattern - lowest) % total_rows
    picked = jnp.take(extended, positions, axis=1)
    product = jnp.einsum("vrkc,rkdc->vrd", picked, block_tiles, precision=lax.Precision.HIGHEST)
    return product.reshape(vec_count, local_rows * tile_width)


def lower_solve(factor, right_side):
    return lax.linalg.triangular_solve(factor, right_side, left_side=True, lower=True)


def local(block_tiles, tile_pattern, start_vectors, centers, halfwidths, dup_pairs):
    initial = start_vectors[0]
    center = centers[0]
    halfwidth = halfwidths[0]
    order_total = initial.shape[1] * lax.axis_size("row")
    previous = initial
    current = (apply_local(initial, block_tiles, tile_pattern) - center * initial) / halfwidth
    for degree in range(DEG - 1):
        following = (
            2.0 * (apply_local(current, block_tiles, tile_pattern) - center * current) / halfwidth
            - previous
        )
        previous, current = (current, following)
    gram_matrix = lax.psum(jnp.dot(current, current.T, precision=lax.Precision.HIGHEST), "row")
    factor = jnp.linalg.cholesky(gram_matrix)
    basis_raw = math.sqrt(order_total) * lower_solve(factor, current)
    imaged = apply_local(basis_raw, block_tiles, tile_pattern)
    projected = (
        lax.psum(jnp.dot(basis_raw, imaged.T, precision=lax.Precision.HIGHEST), "row") / order_total
    )
    vec_count = basis_raw.shape[0]
    columns = jnp.arange(vec_count, dtype=jnp.int32)
    own_index = dup_pairs[0, :, 0]
    their_index = dup_pairs[0, :, 1]
    target_mask = (own_index[:, None] == columns[None, :]).astype(jnp.float32)
    lower_basis = from_behind_2(basis_raw, "cuts", 1)
    selector = (their_index[:, None] == columns[None, :]).astype(jnp.float32)
    lower_rows = jnp.dot(selector, lower_basis, precision=lax.Precision.HIGHEST)
    correlation = (
        lax.psum(jnp.dot(lower_rows, basis_raw.T, precision=lax.Precision.HIGHEST), "row")
        / order_total
    )
    filtered_basis = basis_raw - jnp.dot(
        (target_mask * correlation).T, lower_rows, precision=lax.Precision.HIGHEST
    )
    return (filtered_basis[None], projected[None])


def solution(mesh):
    in_specs = (
        P("row", None, None, None),
        P("row", None),
        P("cuts", None, "row"),
        P("cuts"),
        P("cuts"),
        P("cuts", None, None),
    )
    out_specs = (P("cuts", None, "row"), P("cuts", None, None))
    return jax.shard_map(local, mesh=mesh, in_specs=in_specs, out_specs=out_specs, check_vma=False)
```

profile of v0, /device:TPU:1, one launch (start us, length us, event | category | flops | bytes accessed | tf_op | source)
XLA Modules:
  0.0 857.7 jit_solution(17012417078433444619)
XLA Ops:
  0.6 6.6 collective-permute-start
  7.3 7.9 collective-permute-start.1
  15.1 3.1 collective-permute-start.2
  20.2 2.4 collective-permute-start.4
  25.5 5.5 collective-permute-start.5
  33.2 5.8 collective-permute-start.7
  41.7 6.7 fusion.16
  48.4 4.1 collective-permute-start.8
  52.5 2.8 collective-permute-start.9
  57.5 2.2 collective-permute-start.11
  61.9 6.5 collective-permute-start.13
  68.4 4.7 collective-permute-start.14
  73.2 3.8 collective-permute-start.15
  77.1 3.0 collective-permute-done.15
  80.8 6.7 fusion.14
  87.6 2.3 collective-permute-start.16
  89.9 3.3 collective-permute-start.17
  95.1 2.5 collective-permute-start.19
  99.5 6.6 collective-permute-start.21
  106.2 4.9 collective-permute-start.22
  111.1 4.4 collective-permute-start.23
  115.6 2.8 collective-permute-done.23
  119.2 6.7 fusion.12
  127.8 2.6 collective-permute-start.25
  132.3 2.5 collective-permute-start.27
  136.7 6.7 collective-permute-start.29
  143.5 4.7 collective-permute-start.30
  148.2 5.7 collective-permute-start.31
  156.2 6.7 fusion.10
  165.0 3.3 collective-permute-start.33
  170.2 2.5 collective-permute-start.35
  174.7 6.6 collective-permute-start.37
  181.3 4.8 collective-permute-start.38
  186.2 5.6 collective-permute-start.39
  194.2 6.7 fusion.8
  202.9 3.0 collective-permute-start.41
  207.8 2.5 collective-permute-start.43
  212.2 6.6 collective-permute-start.45
  218.8 4.6 collective-permute-start.46
  223.5 5.8 collective-permute-start.47
  231.5 6.7 fusion.6
  240.2 3.5 collective-permute-start.49
  245.6 2.5 collective-permute-start.51
  250.0 6.6 collective-permute-start.53
  256.6 4.6 collective-permute-start.54
  261.2 5.6 collective-permute-start.55
  269.5 6.7 fusion.4
  278.1 3.1 collective-permute-start.57
  283.1 2.5 collective-permute-start.59
  287.6 6.6 collective-permute-start.61
  294.2 4.6 collective-permute-start.62
  298.8 5.8 collective-permute-start.63
  307.0 7.2 fusion.43
  314.4 245.9 %psum.21 = f32[32,32]{0,1:T(8,128)S(1)} all-reduce(f32[32,32]{0,1:T(8,128)S(1)} %convolution_bitcast_fusion), channel_id=1, replica_groups=mesh['cuts'=8,'row'=64] {'row'}, use_global_device_ids=true, to_apply=%region_0.2 | all-reduce | flops 1024 | bytes 8192 | tf_op jit(solution)/shard_map/psum | solution.py:62
  560.4 2.9 cholesky.16
  564.7 2.4 custom-call.6
  573.2 3.6 collective-permute-start.68
  576.8 5.9 collective-permute-start.69
  582.7 7.0 collective-permute-start.70
  589.7 5.0 collective-permute-start.71
  594.7 5.5 collective-permute-start.72
  600.2 3.1 collective-permute-start.64
  604.2 6.7 fusion.30
  611.4 244.7 %all-reduce = (f32[8,32]{1,0:T(8,128)S(1)}, f32[32,32]{1,0:T(8,128)S(1)}) all-reduce(f32[8,32]{1,0:T(8,128)S(1)} %fusion.129, f32[32,32]{1,0:T(8,128)S(1)} %fusion.64), channel_id=1, replica_groups=mesh['cuts'=8,'row'=64] {'row'}, use_global_device_ids=true, to_apply=%region_3.5 | all-reduce | flops 1280 | bytes 10240 | tf_op jit(solution)/shard_map/psum | solution.py:78
  (221 shorter events, 69.0 us)
Async XLA Ops:
  0.6 24.9 %collective-permute-start = (f32[32,384]{1,0:T(8,128)}, f32[32,384]{1,0:T(8,128)S(1)}, u32[]{:S(2)}, u32[]{:S(2)}) collective-permute-start(f32[32,384]{1,0:T(8,128)} %bitcast.384), channel_id=1, source_target_pairs={{0,4},{1,5},{2,6},{3,7},{4,8},{5,9},{6,10},{7,11},{8,12},{9,13},{1... | collective-permute-start | bytes 147464 | tf_op jit(solution)/shard_map/ppermute | solution.py:14
  7.3 23.8 %collective-permute-start.1 = (f32[32,384]{1,0:T(8,128)}, f32[32,384]{1,0:T(8,128)S(1)}, u32[]{:S(2)}, u32[]{:S(2)}) collective-permute-start(f32[32,384]{1,0:T(8,128)} %bitcast.385), channel_id=1, source_target_pairs={{0,3},{1,4},{2,5},{3,6},{4,7},{5,8},{6,9},{7,10},{8,11},{9,12},{10... | collective-permute-start | bytes 147464 | tf_op jit(solution)/shard_map/ppermute | solution.py:14
  15.1 18.0 %collective-permute-start.2 = (f32[32,384]{1,0:T(8,128)}, f32[32,384]{1,0:T(8,128)S(1)}, u32[]{:S(2)}, u32[]{:S(2)}) collective-permute-start(f32[32,384]{1,0:T(8,128)} %bitcast.386), channel_id=1, source_target_pairs={{0,2},{1,3},{2,4},{3,5},{4,6},{5,7},{6,8},{7,9},{8,10},{9,11},{10,... | collective-permute-start | bytes 147464 | tf_op jit(solution)/shard_map/ppermute | solution.py:14
  18.2 20.7 %collective-permute-start.3 = (f32[32,384]{1,0:T(8,128)}, f32[32,384]{1,0:T(8,128)S(1)}, u32[]{:S(2)}, u32[]{:S(2)}) collective-permute-start(f32[32,384]{1,0:T(8,128)} %bitcast.387), channel_id=1, source_target_pairs={{0,1},{1,2},{2,3},{3,4},{4,5},{5,6},{6,7},{7,8},{8,9},{9,10},{10,1... | collective-permute-start | bytes 147464 | tf_op jit(solution)/shard_map/ppermute | solution.py:14
  20.2 18.8 %collective-permute-start.4 = (f32[32,384]{1,0:T(8,128)}, f32[32,384]{1,0:T(8,128)S(1)}, u32[]{:S(2)}, u32[]{:S(2)}) collective-permute-start(f32[32,384]{1,0:T(8,128)} %bitcast.388), channel_id=1, source_target_pairs={{0,63},{1,0},{2,1},{3,2},{4,3},{5,4},{6,5},{7,6},{8,7},{9,8},{10,9... | collective-permute-start | bytes 147464 | tf_op jit(solution)/shard_map/ppermute | solution.py:14
  25.5 13.5 %collective-permute-start.5 = (f32[32,384]{1,0:T(8,128)}, f32[32,384]{1,0:T(8,128)S(1)}, u32[]{:S(2)}, u32[]{:S(2)}) collective-permute-start(f32[32,384]{1,0:T(8,128)} %bitcast.389), channel_id=1, source_target_pairs={{0,62},{1,63},{2,0},{3,1},{4,2},{5,3},{6,4},{7,5},{8,6},{9,7},{10,... | collective-permute-start | bytes 147464 | tf_op jit(solution)/shard_map/ppermute | solution.py:14
  48.4 13.4 %collective-permute-start.8 = (f32[32,384]{1,0:T(8,128)S(1)}, f32[32,384]{1,0:T(8,128)S(1)}, u32[]{:S(2)}, u32[]{:S(2)}) collective-permute-start(f32[32,384]{1,0:T(8,128)S(1)} %fusion.87), channel_id=1, source_target_pairs={{0,4},{1,5},{2,6},{3,7},{4,8},{5,9},{6,10},{7,11},{8,12},{9,13},{1... | collective-permute-start | bytes 147464 | tf_op jit(solution)/shard_map/ppermute | solution.py:14
  52.5 15.9 %collective-permute-start.9 = (f32[32,384]{1,0:T(8,128)S(1)}, f32[32,384]{1,0:T(8,128)S(1)}, u32[]{:S(2)}, u32[]{:S(2)}) collective-permute-start(f32[32,384]{1,0:T(8,128)S(1)} %fusion.87), channel_id=1, source_target_pairs={{0,3},{1,4},{2,5},{3,6},{4,7},{5,8},{6,9},{7,10},{8,11},{9,12},{10... | collective-permute-start | bytes 147464 | tf_op jit(solution)/shard_map/ppermute | solution.py:14
  55.3 17.8 %collective-permute-start.10 = (f32[32,384]{1,0:T(8,128)S(1)}, f32[32,384]{1,0:T(8,128)S(1)}, u32[]{:S(2)}, u32[]{:S(2)}) collective-permute-start(f32[32,384]{1,0:T(8,128)S(1)} %fusion.87), channel_id=1, source_target_pairs={{0,2},{1,3},{2,4},{3,5},{4,6},{5,7},{6,8},{7,9},{8,10},{9,11},{10,... | collective-permute-start | bytes 147464 | tf_op jit(solution)/shard_map/ppermute | solution.py:14
  57.5 19.5 %collective-permute-start.11 = (f32[32,384]{1,0:T(8,128)S(1)}, f32[32,384]{1,0:T(8,128)S(1)}, u32[]{:S(2)}, u32[]{:S(2)}) collective-permute-start(f32[32,384]{1,0:T(8,128)S(1)} %fusion.87), channel_id=1, source_target_pairs={{0,1},{1,2},{2,3},{3,4},{4,5},{5,6},{6,7},{7,8},{8,9},{9,10},{10,1... | collective-permute-start | bytes 147464 | tf_op jit(solution)/shard_map/ppermute | solution.py:14
  59.8 17.3 %collective-permute-start.12 = (f32[32,384]{1,0:T(8,128)S(1)}, f32[32,384]{1,0:T(8,128)S(1)}, u32[]{:S(2)}, u32[]{:S(2)}) collective-permute-start(f32[32,384]{1,0:T(8,128)S(1)} %fusion.87), channel_id=1, source_target_pairs={{0,63},{1,0},{2,1},{3,2},{4,3},{5,4},{6,5},{7,6},{8,7},{9,8},{10,9... | collective-permute-start | bytes 147464 | tf_op jit(solution)/shard_map/ppermute | solution.py:14
  61.9 15.2 %collective-permute-start.13 = (f32[32,384]{1,0:T(8,128)S(1)}, f32[32,384]{1,0:T(8,128)S(1)}, u32[]{:S(2)}, u32[]{:S(2)}) collective-permute-start(f32[32,384]{1,0:T(8,128)S(1)} %fusion.87), channel_id=1, source_target_pairs={{0,62},{1,63},{2,0},{3,1},{4,2},{5,3},{6,4},{7,5},{8,6},{9,7},{10,... | collective-permute-start | bytes 147464 | tf_op jit(solution)/shard_map/ppermute | solution.py:14
  68.4 8.7 %collective-permute-start.14 = (f32[32,384]{1,0:T(8,128)S(1)}, f32[32,384]{1,0:T(8,128)S(1)}, u32[]{:S(2)}, u32[]{:S(2)}) collective-permute-start(f32[32,384]{1,0:T(8,128)S(1)} %fusion.87), channel_id=1, source_target_pairs={{0,61},{1,62},{2,63},{3,0},{4,1},{5,2},{6,3},{7,4},{8,5},{9,6},{10... | collective-permute-start | bytes 147464 | tf_op jit(solution)/shard_map/ppermute | solution.py:14
  87.6 12.0 %collective-permute-start.16 = (f32[32,384]{1,0:T(8,128)S(1)}, f32[32,384]{1,0:T(8,128)S(1)}, u32[]{:S(2)}, u32[]{:S(2)}) collective-permute-start(f32[32,384]{1,0:T(8,128)S(1)} %fusion.86), channel_id=1, source_target_pairs={{0,4},{1,5},{2,6},{3,7},{4,8},{5,9},{6,10},{7,11},{8,12},{9,13},{1... | collective-permute-start | bytes 147464 | tf_op jit(solution)/shard_map/ppermute | solution.py:14
  89.9 16.3 %collective-permute-start.17 = (f32[32,384]{1,0:T(8,128)S(1)}, f32[32,384]{1,0:T(8,128)S(1)}, u32[]{:S(2)}, u32[]{:S(2)}) collective-permute-start(f32[32,384]{1,0:T(8,128)S(1)} %fusion.86), channel_id=1, source_target_pairs={{0,3},{1,4},{2,5},{3,6},{4,7},{5,8},{6,9},{7,10},{8,11},{9,12},{10... | collective-permute-start | bytes 147464 | tf_op jit(solution)/shard_map/ppermute | solution.py:14
  93.2 17.9 %collective-permute-start.18 = (f32[32,384]{1,0:T(8,128)S(1)}, f32[32,384]{1,0:T(8,128)S(1)}, u32[]{:S(2)}, u32[]{:S(2)}) collective-permute-start(f32[32,384]{1,0:T(8,128)S(1)} %fusion.86), channel_id=1, source_target_pairs={{0,2},{1,3},{2,4},{3,5},{4,6},{5,7},{6,8},{7,9},{8,10},{9,11},{10,... | collective-permute-start | bytes 147464 | tf_op jit(solution)/shard_map/ppermute | solution.py:14
  95.1 20.4 %collective-permute-start.19 = (f32[32,384]{1,0:T(8,128)S(1)}, f32[32,384]{1,0:T(8,128)S(1)}, u32[]{:S(2)}, u32[]{:S(2)}) collective-permute-start(f32[32,384]{1,0:T(8,128)S(1)} %fusion.86), channel_id=1, source_target_pairs={{0,1},{1,2},{2,3},{3,4},{4,5},{5,6},{6,7},{7,8},{8,9},{9,10},{10,1... | collective-permute-start | bytes 147464 | tf_op jit(solution)/shard_map/ppermute | solution.py:14
  97.6 18.0 %collective-permute-start.20 = (f32[32,384]{1,0:T(8,128)S(1)}, f32[32,384]{1,0:T(8,128)S(1)}, u32[]{:S(2)}, u32[]{:S(2)}) collective-permute-start(f32[32,384]{1,0:T(8,128)S(1)} %fusion.86), channel_id=1, source_target_pairs={{0,63},{1,0},{2,1},{3,2},{4,3},{5,4},{6,5},{7,6},{8,7},{9,8},{10,9... | collective-permute-start | bytes 147464 | tf_op jit(solution)/shard_map/ppermute | solution.py:14
  99.5 16.0 %collective-permute-start.21 = (f32[32,384]{1,0:T(8,128)S(1)}, f32[32,384]{1,0:T(8,128)S(1)}, u32[]{:S(2)}, u32[]{:S(2)}) collective-permute-start(f32[32,384]{1,0:T(8,128)S(1)} %fusion.86), channel_id=1, source_target_pairs={{0,62},{1,63},{2,0},{3,1},{4,2},{5,3},{6,4},{7,5},{8,6},{9,7},{10,... | collective-permute-start | bytes 147464 | tf_op jit(solution)/shard_map/ppermute | solution.py:14
  106.2 9.4 %collective-permute-start.22 = (f32[32,384]{1,0:T(8,128)S(1)}, f32[32,384]{1,0:T(8,128)S(1)}, u32[]{:S(2)}, u32[]{:S(2)}) collective-permute-start(f32[32,384]{1,0:T(8,128)S(1)} %fusion.86), channel_id=1, source_target_pairs={{0,61},{1,62},{2,63},{3,0},{4,1},{5,2},{6,3},{7,4},{8,5},{9,6},{10... | collective-permute-start | bytes 147464 | tf_op jit(solution)/shard_map/ppermute | solution.py:14
  125.9 10.8 %collective-permute-start.24 = (f32[32,384]{1,0:T(8,128)S(1)}, f32[32,384]{1,0:T(8,128)S(1)}, u32[]{:S(2)}, u32[]{:S(2)}) collective-permute-start(f32[32,384]{1,0:T(8,128)S(1)} %fusion.83), channel_id=1, source_target_pairs={{0,4},{1,5},{2,6},{3,7},{4,8},{5,9},{6,10},{7,11},{8,12},{9,13},{1... | collective-permute-start | bytes 147464 | tf_op jit(solution)/shard_map/ppermute | solution.py:14
  127.8 15.6 %collective-permute-start.25 = (f32[32,384]{1,0:T(8,128)S(1)}, f32[32,384]{1,0:T(8,128)S(1)}, u32[]{:S(2)}, u32[]{:S(2)}) collective-permute-start(f32[32,384]{1,0:T(8,128)S(1)} %fusion.83), channel_id=1, source_target_pairs={{0,3},{1,4},{2,5},{3,6},{4,7},{5,8},{6,9},{7,10},{8,11},{9,12},{10... | collective-permute-start | bytes 147464 | tf_op jit(solution)/shard_map/ppermute | solution.py:14
  130.4 17.8 %collective-permute-start.26 = (f32[32,384]{1,0:T(8,128)S(1)}, f32[32,384]{1,0:T(8,128)S(1)}, u32[]{:S(2)}, u32[]{:S(2)}) collective-permute-start(f32[32,384]{1,0:T(8,128)S(1)} %fusion.83), channel_id=1, source_target_pairs={{0,2},{1,3},{2,4},{3,5},{4,6},{5,7},{6,8},{7,9},{8,10},{9,11},{10,... | collective-permute-start | bytes 147464 | tf_op jit(solution)/shard_map/ppermute | solution.py:14
  132.3 21.7 %collective-permute-start.27 = (f32[32,384]{1,0:T(8,128)S(1)}, f32[32,384]{1,0:T(8,128)S(1)}, u32[]{:S(2)}, u32[]{:S(2)}) collective-permute-start(f32[32,384]{1,0:T(8,128)S(1)} %fusion.83), channel_id=1, source_target_pairs={{0,1},{1,2},{2,3},{3,4},{4,5},{5,6},{6,7},{7,8},{8,9},{9,10},{10,1... | collective-permute-start | bytes 147464 | tf_op jit(solution)/shard_map/ppermute | solution.py:14
  134.8 19.2 %collective-permute-start.28 = (f32[32,384]{1,0:T(8,128)S(1)}, f32[32,384]{1,0:T(8,128)S(1)}, u32[]{:S(2)}, u32[]{:S(2)}) collective-permute-start(f32[32,384]{1,0:T(8,128)S(1)} %fusion.83), channel_id=1, source_target_pairs={{0,63},{1,0},{2,1},{3,2},{4,3},{5,4},{6,5},{7,6},{8,7},{9,8},{10,9... | collective-permute-start | bytes 147464 | tf_op jit(solution)/shard_map/ppermute | solution.py:14
  136.7 17.3 %collective-permute-start.29 = (f32[32,384]{1,0:T(8,128)S(1)}, f32[32,384]{1,0:T(8,128)S(1)}, u32[]{:S(2)}, u32[]{:S(2)}) collective-permute-start(f32[32,384]{1,0:T(8,128)S(1)} %fusion.83), channel_id=1, source_target_pairs={{0,62},{1,63},{2,0},{3,1},{4,2},{5,3},{6,4},{7,5},{8,6},{9,7},{10,... | collective-permute-start | bytes 147464 | tf_op jit(solution)/shard_map/ppermute | solution.py:14
  143.5 10.6 %collective-permute-start.30 = (f32[32,384]{1,0:T(8,128)S(1)}, f32[32,384]{1,0:T(8,128)S(1)}, u32[]{:S(2)}, u32[]{:S(2)}) collective-permute-start(f32[32,384]{1,0:T(8,128)S(1)} %fusion.83), channel_id=1, source_target_pairs={{0,61},{1,62},{2,63},{3,0},{4,1},{5,2},{6,3},{7,4},{8,5},{9,6},{10... | collective-permute-start | bytes 147464 | tf_op jit(solution)/shard_map/ppermute | solution.py:14
  163.0 11.7 %collective-permute-start.32 = (f32[32,384]{1,0:T(8,128)S(1)}, f32[32,384]{1,0:T(8,128)S(1)}, u32[]{:S(2)}, u32[]{:S(2)}) collective-permute-start(f32[32,384]{1,0:T(8,128)S(1)} %fusion.80), channel_id=1, source_target_pairs={{0,4},{1,5},{2,6},{3,7},{4,8},{5,9},{6,10},{7,11},{8,12},{9,13},{1... | collective-permute-start | bytes 147464 | tf_op jit(solution)/shard_map/ppermute | solution.py:14
  165.0 16.3 %collective-permute-start.33 = (f32[32,384]{1,0:T(8,128)S(1)}, f32[32,384]{1,0:T(8,128)S(1)}, u32[]{:S(2)}, u32[]{:S(2)}) collective-permute-start(f32[32,384]{1,0:T(8,128)S(1)} %fusion.80), channel_id=1, source_target_pairs={{0,3},{1,4},{2,5},{3,6},{4,7},{5,8},{6,9},{7,10},{8,11},{9,12},{10... | collective-permute-start | bytes 147464 | tf_op jit(solution)/shard_map/ppermute | solution.py:14
  168.3 17.9 %collective-permute-start.34 = (f32[32,384]{1,0:T(8,128)S(1)}, f32[32,384]{1,0:T(8,128)S(1)}, u32[]{:S(2)}, u32[]{:S(2)}) collective-permute-start(f32[32,384]{1,0:T(8,128)S(1)} %fusion.80), channel_id=1, source_target_pairs={{0,2},{1,3},{2,4},{3,5},{4,6},{5,7},{6,8},{7,9},{8,10},{9,11},{10,... | collective-permute-start | bytes 147464 | tf_op jit(solution)/shard_map/ppermute | solution.py:14
  170.2 21.6 %collective-permute-start.35 = (f32[32,384]{1,0:T(8,128)S(1)}, f32[32,384]{1,0:T(8,128)S(1)}, u32[]{:S(2)}, u32[]{:S(2)}) collective-permute-start(f32[32,384]{1,0:T(8,128)S(1)} %fusion.80), channel_id=1, source_target_pairs={{0,1},{1,2},{2,3},{3,4},{4,5},{5,6},{6,7},{7,8},{8,9},{9,10},{10,1... | collective-permute-start | bytes 147464 | tf_op jit(solution)/shard_map/ppermute | solution.py:14
  172.7 19.2 %collective-permute-start.36 = (f32[32,384]{1,0:T(8,128)S(1)}, f32[32,384]{1,0:T(8,128)S(1)}, u32[]{:S(2)}, u32[]{:S(2)}) collective-permute-start(f32[32,384]{1,0:T(8,128)S(1)} %fusion.80), channel_id=1, source_target_pairs={{0,63},{1,0},{2,1},{3,2},{4,3},{5,4},{6,5},{7,6},{8,7},{9,8},{10,9... | collective-permute-start | bytes 147464 | tf_op jit(solution)/shard_map/ppermute | solution.py:14
  174.7 17.3 %collective-permute-start.37 = (f32[32,384]{1,0:T(8,128)S(1)}, f32[32,384]{1,0:T(8,128)S(1)}, u32[]{:S(2)}, u32[]{:S(2)}) collective-permute-start(f32[32,384]{1,0:T(8,128)S(1)} %fusion.80), channel_id=1, source_target_pairs={{0,62},{1,63},{2,0},{3,1},{4,2},{5,3},{6,4},{7,5},{8,6},{9,7},{10,... | collective-permute-start | bytes 147464 | tf_op jit(solution)/shard_map/ppermute | solution.py:14
  181.3 10.6 %collective-permute-start.38 = (f32[32,384]{1,0:T(8,128)S(1)}, f32[32,384]{1,0:T(8,128)S(1)}, u32[]{:S(2)}, u32[]{:S(2)}) collective-permute-start(f32[32,384]{1,0:T(8,128)S(1)} %fusion.80), channel_id=1, source_target_pairs={{0,61},{1,62},{2,63},{3,0},{4,1},{5,2},{6,3},{7,4},{8,5},{9,6},{10... | collective-permute-start | bytes 147464 | tf_op jit(solution)/shard_map/ppermute | solution.py:14
  201.0 11.2 %collective-permute-start.40 = (f32[32,384]{1,0:T(8,128)S(1)}, f32[32,384]{1,0:T(8,128)S(1)}, u32[]{:S(2)}, u32[]{:S(2)}) collective-permute-start(f32[32,384]{1,0:T(8,128)S(1)} %fusion.77), channel_id=1, source_target_pairs={{0,4},{1,5},{2,6},{3,7},{4,8},{5,9},{6,10},{7,11},{8,12},{9,13},{1... | collective-permute-start | bytes 147464 | tf_op jit(solution)/shard_map/ppermute | solution.py:14
  202.9 16.0 %collective-permute-start.41 = (f32[32,384]{1,0:T(8,128)S(1)}, f32[32,384]{1,0:T(8,128)S(1)}, u32[]{:S(2)}, u32[]{:S(2)}) collective-permute-start(f32[32,384]{1,0:T(8,128)S(1)} %fusion.77), channel_id=1, source_target_pairs={{0,3},{1,4},{2,5},{3,6},{4,7},{5,8},{6,9},{7,10},{8,11},{9,12},{10... | collective-permute-start | bytes 147464 | tf_op jit(solution)/shard_map/ppermute | solution.py:14
  205.9 17.6 %collective-permute-start.42 = (f32[32,384]{1,0:T(8,128)S(1)}, f32[32,384]{1,0:T(8,128)S(1)}, u32[]{:S(2)}, u32[]{:S(2)}) collective-permute-start(f32[32,384]{1,0:T(8,128)S(1)} %fusion.77), channel_id=1, source_target_pairs={{0,2},{1,3},{2,4},{3,5},{4,6},{5,7},{6,8},{7,9},{8,10},{9,11},{10,... | collective-permute-start | bytes 147464 | tf_op jit(solution)/shard_map/ppermute | solution.py:14
  207.8 21.5 %collective-permute-start.43 = (f32[32,384]{1,0:T(8,128)S(1)}, f32[32,384]{1,0:T(8,128)S(1)}, u32[]{:S(2)}, u32[]{:S(2)}) collective-permute-start(f32[32,384]{1,0:T(8,128)S(1)} %fusion.77), channel_id=1, source_target_pairs={{0,1},{1,2},{2,3},{3,4},{4,5},{5,6},{6,7},{7,8},{8,9},{9,10},{10,1... | collective-permute-start | bytes 147464 | tf_op jit(solution)/shard_map/ppermute | solution.py:14
  210.3 19.0 %collective-permute-start.44 = (f32[32,384]{1,0:T(8,128)S(1)}, f32[32,384]{1,0:T(8,128)S(1)}, u32[]{:S(2)}, u32[]{:S(2)}) collective-permute-start(f32[32,384]{1,0:T(8,128)S(1)} %fusion.77), channel_id=1, source_target_pairs={{0,63},{1,0},{2,1},{3,2},{4,3},{5,4},{6,5},{7,6},{8,7},{9,8},{10,9... | collective-permute-start | bytes 147464 | tf_op jit(solution)/shard_map/ppermute | solution.py:14
  212.2 17.1 %collective-permute-start.45 = (f32[32,384]{1,0:T(8,128)S(1)}, f32[32,384]{1,0:T(8,128)S(1)}, u32[]{:S(2)}, u32[]{:S(2)}) collective-permute-start(f32[32,384]{1,0:T(8,128)S(1)} %fusion.77), channel_id=1, source_target_pairs={{0,62},{1,63},{2,0},{3,1},{4,2},{5,3},{6,4},{7,5},{8,6},{9,7},{10,... | collective-permute-start | bytes 147464 | tf_op jit(solution)/shard_map/ppermute | solution.py:14
  218.8 10.5 %collective-permute-start.46 = (f32[32,384]{1,0:T(8,128)S(1)}, f32[32,384]{1,0:T(8,128)S(1)}, u32[]{:S(2)}, u32[]{:S(2)}) collective-permute-start(f32[32,384]{1,0:T(8,128)S(1)} %fusion.77), channel_id=1, source_target_pairs={{0,61},{1,62},{2,63},{3,0},{4,1},{5,2},{6,3},{7,4},{8,5},{9,6},{10... | collective-permute-start | bytes 147464 | tf_op jit(solution)/shard_map/ppermute | solution.py:14
  238.2 11.7 %collective-permute-start.48 = (f32[32,384]{1,0:T(8,128)S(1)}, f32[32,384]{1,0:T(8,128)S(1)}, u32[]{:S(2)}, u32[]{:S(2)}) collective-permute-start(f32[32,384]{1,0:T(8,128)S(1)} %fusion.74), channel_id=1, source_target_pairs={{0,4},{1,5},{2,6},{3,7},{4,8},{5,9},{6,10},{7,11},{8,12},{9,13},{1... | collective-permute-start | bytes 147464 | tf_op jit(solution)/shard_map/ppermute | solution.py:14
  240.2 16.4 %collective-permute-start.49 = (f32[32,384]{1,0:T(8,128)S(1)}, f32[32,384]{1,0:T(8,128)S(1)}, u32[]{:S(2)}, u32[]{:S(2)}) collective-permute-start(f32[32,384]{1,0:T(8,128)S(1)} %fusion.74), channel_id=1, source_target_pairs={{0,3},{1,4},{2,5},{3,6},{4,7},{5,8},{6,9},{7,10},{8,11},{9,12},{10... | collective-permute-start | bytes 147464 | tf_op jit(solution)/shard_map/ppermute | solution.py:14
  243.6 17.6 %collective-permute-start.50 = (f32[32,384]{1,0:T(8,128)S(1)}, f32[32,384]{1,0:T(8,128)S(1)}, u32[]{:S(2)}, u32[]{:S(2)}) collective-permute-start(f32[32,384]{1,0:T(8,128)S(1)} %fusion.74), channel_id=1, source_target_pairs={{0,2},{1,3},{2,4},{3,5},{4,6},{5,7},{6,8},{7,9},{8,10},{9,11},{10,... | collective-permute-start | bytes 147464 | tf_op jit(solution)/shard_map/ppermute | solution.py:14
  245.6 21.3 %collective-permute-start.51 = (f32[32,384]{1,0:T(8,128)S(1)}, f32[32,384]{1,0:T(8,128)S(1)}, u32[]{:S(2)}, u32[]{:S(2)}) collective-permute-start(f32[32,384]{1,0:T(8,128)S(1)} %fusion.74), channel_id=1, source_target_pairs={{0,1},{1,2},{2,3},{3,4},{4,5},{5,6},{6,7},{7,8},{8,9},{9,10},{10,1... | collective-permute-start | bytes 147464 | tf_op jit(solution)/shard_map/ppermute | solution.py:14
  248.0 18.8 %collective-permute-start.52 = (f32[32,384]{1,0:T(8,128)S(1)}, f32[32,384]{1,0:T(8,128)S(1)}, u32[]{:S(2)}, u32[]{:S(2)}) collective-permute-start(f32[32,384]{1,0:T(8,128)S(1)} %fusion.74), channel_id=1, source_target_pairs={{0,63},{1,0},{2,1},{3,2},{4,3},{5,4},{6,5},{7,6},{8,7},{9,8},{10,9... | collective-permute-start | bytes 147464 | tf_op jit(solution)/shard_map/ppermute | solution.py:14
  250.0 16.9 %collective-permute-start.53 = (f32[32,384]{1,0:T(8,128)S(1)}, f32[32,384]{1,0:T(8,128)S(1)}, u32[]{:S(2)}, u32[]{:S(2)}) collective-permute-start(f32[32,384]{1,0:T(8,128)S(1)} %fusion.74), channel_id=1, source_target_pairs={{0,62},{1,63},{2,0},{3,1},{4,2},{5,3},{6,4},{7,5},{8,6},{9,7},{10,... | collective-permute-start | bytes 147464 | tf_op jit(solution)/shard_map/ppermute | solution.py:14
  256.6 10.3 %collective-permute-start.54 = (f32[32,384]{1,0:T(8,128)S(1)}, f32[32,384]{1,0:T(8,128)S(1)}, u32[]{:S(2)}, u32[]{:S(2)}) collective-permute-start(f32[32,384]{1,0:T(8,128)S(1)} %fusion.74), channel_id=1, source_target_pairs={{0,61},{1,62},{2,63},{3,0},{4,1},{5,2},{6,3},{7,4},{8,5},{9,6},{10... | collective-permute-start | bytes 147464 | tf_op jit(solution)/shard_map/ppermute | solution.py:14
  276.2 11.3 %collective-permute-start.56 = (f32[32,384]{1,0:T(8,128)S(1)}, f32[32,384]{1,0:T(8,128)S(1)}, u32[]{:S(2)}, u32[]{:S(2)}) collective-permute-start(f32[32,384]{1,0:T(8,128)S(1)} %fusion.71), channel_id=1, source_target_pairs={{0,4},{1,5},{2,6},{3,7},{4,8},{5,9},{6,10},{7,11},{8,12},{9,13},{1... | collective-permute-start | bytes 147464 | tf_op jit(solution)/shard_map/ppermute | solution.py:14
  278.1 16.1 %collective-permute-start.57 = (f32[32,384]{1,0:T(8,128)S(1)}, f32[32,384]{1,0:T(8,128)S(1)}, u32[]{:S(2)}, u32[]{:S(2)}) collective-permute-start(f32[32,384]{1,0:T(8,128)S(1)} %fusion.71), channel_id=1, source_target_pairs={{0,3},{1,4},{2,5},{3,6},{4,7},{5,8},{6,9},{7,10},{8,11},{9,12},{10... | collective-permute-start | bytes 147464 | tf_op jit(solution)/shard_map/ppermute | solution.py:14
  281.2 17.6 %collective-permute-start.58 = (f32[32,384]{1,0:T(8,128)S(1)}, f32[32,384]{1,0:T(8,128)S(1)}, u32[]{:S(2)}, u32[]{:S(2)}) collective-permute-start(f32[32,384]{1,0:T(8,128)S(1)} %fusion.71), channel_id=1, source_target_pairs={{0,2},{1,3},{2,4},{3,5},{4,6},{5,7},{6,8},{7,9},{8,10},{9,11},{10,... | collective-permute-start | bytes 147464 | tf_op jit(solution)/shard_map/ppermute | solution.py:14
  283.1 21.4 %collective-permute-start.59 = (f32[32,384]{1,0:T(8,128)S(1)}, f32[32,384]{1,0:T(8,128)S(1)}, u32[]{:S(2)}, u32[]{:S(2)}) collective-permute-start(f32[32,384]{1,0:T(8,128)S(1)} %fusion.71), channel_id=1, source_target_pairs={{0,1},{1,2},{2,3},{3,4},{4,5},{5,6},{6,7},{7,8},{8,9},{9,10},{10,1... | collective-permute-start | bytes 147464 | tf_op jit(solution)/shard_map/ppermute | solution.py:14
  285.6 19.0 %collective-permute-start.60 = (f32[32,384]{1,0:T(8,128)S(1)}, f32[32,384]{1,0:T(8,128)S(1)}, u32[]{:S(2)}, u32[]{:S(2)}) collective-permute-start(f32[32,384]{1,0:T(8,128)S(1)} %fusion.71), channel_id=1, source_target_pairs={{0,63},{1,0},{2,1},{3,2},{4,3},{5,4},{6,5},{7,6},{8,7},{9,8},{10,9... | collective-permute-start | bytes 147464 | tf_op jit(solution)/shard_map/ppermute | solution.py:14
  287.6 17.1 %collective-permute-start.61 = (f32[32,384]{1,0:T(8,128)S(1)}, f32[32,384]{1,0:T(8,128)S(1)}, u32[]{:S(2)}, u32[]{:S(2)}) collective-permute-start(f32[32,384]{1,0:T(8,128)S(1)} %fusion.71), channel_id=1, source_target_pairs={{0,62},{1,63},{2,0},{3,1},{4,2},{5,3},{6,4},{7,5},{8,6},{9,7},{10,... | collective-permute-start | bytes 147464 | tf_op jit(solution)/shard_map/ppermute | solution.py:14
  294.2 10.5 %collective-permute-start.62 = (f32[32,384]{1,0:T(8,128)S(1)}, f32[32,384]{1,0:T(8,128)S(1)}, u32[]{:S(2)}, u32[]{:S(2)}) collective-permute-start(f32[32,384]{1,0:T(8,128)S(1)} %fusion.71), channel_id=1, source_target_pairs={{0,61},{1,62},{2,63},{3,0},{4,1},{5,2},{6,3},{7,4},{8,5},{9,6},{10... | collective-permute-start | bytes 147464 | tf_op jit(solution)/shard_map/ppermute | solution.py:14
  567.4 15.3 %collective-permute-start.65 = (f32[32,384]{1,0:T(8,128)S(1)}, f32[32,384]{1,0:T(8,128)S(1)}, u32[]{:S(2)}, u32[]{:S(2)}) collective-permute-start(f32[32,384]{1,0:T(8,128)S(1)} %convolution_multiply_fusion), channel_id=1, source_target_pairs={{0,4},{1,5},{2,6},{3,7},{4,8},{5,9},{6,10},{7,11},{8,12},{9,13},{1... | collective-permute-start | bytes 147464 | tf_op jit(solution)/shard_map/ppermute | solution.py:14
  569.3 20.3 %collective-permute-start.66 = (f32[32,384]{1,0:T(8,128)S(1)}, f32[32,384]{1,0:T(8,128)S(1)}, u32[]{:S(2)}, u32[]{:S(2)}) collective-permute-start(f32[32,384]{1,0:T(8,128)S(1)} %convolution_multiply_fusion), channel_id=1, source_target_pairs={{0,3},{1,4},{2,5},{3,6},{4,7},{5,8},{6,9},{7,10},{8,11},{9,12},{10... | collective-permute-start | bytes 147464 | tf_op jit(solution)/shard_map/ppermute | solution.py:14
  571.2 23.4 %collective-permute-start.67 = (f32[32,384]{1,0:T(8,128)S(1)}, f32[32,384]{1,0:T(8,128)S(1)}, u32[]{:S(2)}, u32[]{:S(2)}) collective-permute-start(f32[32,384]{1,0:T(8,128)S(1)} %convolution_multiply_fusion), channel_id=1, source_target_pairs={{0,2},{1,3},{2,4},{3,5},{4,6},{5,7},{6,8},{7,9},{8,10},{9,11},{10,... | collective-permute-start | bytes 147464 | tf_op jit(solution)/shard_map/ppermute | solution.py:14
  573.2 27.0 %collective-permute-start.68 = (f32[32,384]{1,0:T(8,128)S(1)}, f32[32,384]{1,0:T(8,128)S(1)}, u32[]{:S(2)}, u32[]{:S(2)}) collective-permute-start(f32[32,384]{1,0:T(8,128)S(1)} %convolution_multiply_fusion), channel_id=1, source_target_pairs={{0,1},{1,2},{2,3},{3,4},{4,5},{5,6},{6,7},{7,8},{8,9},{9,10},{10,1... | collective-permute-start | bytes 147464 | tf_op jit(solution)/shard_map/ppermute | solution.py:14
  576.8 26.6 %collective-permute-start.69 = (f32[32,384]{1,0:T(8,128)S(1)}, f32[32,384]{1,0:T(8,128)S(1)}, u32[]{:S(2)}, u32[]{:S(2)}) collective-permute-start(f32[32,384]{1,0:T(8,128)S(1)} %convolution_multiply_fusion), channel_id=1, source_target_pairs={{0,63},{1,0},{2,1},{3,2},{4,3},{5,4},{6,5},{7,6},{8,7},{9,8},{10,9... | collective-permute-start | bytes 147464 | tf_op jit(solution)/shard_map/ppermute | solution.py:14
  582.7 20.7 %collective-permute-start.70 = (f32[32,384]{1,0:T(8,128)S(1)}, f32[32,384]{1,0:T(8,128)S(1)}, u32[]{:S(2)}, u32[]{:S(2)}) collective-permute-start(f32[32,384]{1,0:T(8,128)S(1)} %convolution_multiply_fusion), channel_id=1, source_target_pairs={{0,62},{1,63},{2,0},{3,1},{4,2},{5,3},{6,4},{7,5},{8,6},{9,7},{10,... | collective-permute-start | bytes 147464 | tf_op jit(solution)/shard_map/ppermute | solution.py:14
  589.7 13.7 %collective-permute-start.71 = (f32[32,384]{1,0:T(8,128)S(1)}, f32[32,384]{1,0:T(8,128)S(1)}, u32[]{:S(2)}, u32[]{:S(2)}) collective-permute-start(f32[32,384]{1,0:T(8,128)S(1)} %convolution_multiply_fusion), channel_id=1, source_target_pairs={{0,61},{1,62},{2,63},{3,0},{4,1},{5,2},{6,3},{7,4},{8,5},{9,6},{10... | collective-permute-start | bytes 147464 | tf_op jit(solution)/shard_map/ppermute | solution.py:14
  594.7 8.7 %collective-permute-start.72 = (f32[32,384]{1,0:T(8,128)S(1)}, f32[32,384]{1,0:T(8,128)S(1)}, u32[]{:S(2)}, u32[]{:S(2)}) collective-permute-start(f32[32,384]{1,0:T(8,128)S(1)} %convolution_multiply_fusion), channel_id=1, source_target_pairs={{0,60},{1,61},{2,62},{3,63},{4,0},{5,1},{6,2},{7,3},{8,4},{9,5},{1... | collective-permute-start | bytes 147464 | tf_op jit(solution)/shard_map/ppermute | solution.py:14
  600.2 10.9 %collective-permute-start.64 = (f32[32,384]{1,0:T(8,128)S(1)}, f32[32,384]{1,0:T(8,128)S(1)}, u32[]{:S(2)}, u32[]{:S(2)}) collective-permute-start(f32[32,384]{1,0:T(8,128)S(1)} %convolution_multiply_fusion), channel_id=1, source_target_pairs={{0,64},{64,128},{128,192},{192,256},{256,320},{320,384},{384,448},... | collective-permute-start | bytes 147464 | tf_op jit(solution)/shard_map/ppermute | solution.py:20
  (11 other events, 335.9 us)
where the time goes:
time: 864 us; the launch traced here: 858 us
  blocking collectives  491 us (57%)
  starting transfers between devices  269 us (31%)
  matrix products  62.8 us (7%)
  waiting for transfers between devices  15.6 us (2%)
    ppermute x72, starting transfers between devices, from_behind(): lax.ppermute(shard, axis, [(i, (i + by) % size) for i in range(size)])  266 us
    psum x1, blocking collectives, local(): lax.psum(jnp.dot(current, current.T, precision=lax.Precision.HIGHEST), 'r...  246 us
    psum x1, blocking collectives, local(): lax.psum(jnp.dot(lower_rows, basis_raw.T, precision=lax.Precision.HIGHEST...  245 us
    dot_general x9, matrix products, apply_local(): jnp.einsum('vrkc,rkdc->vrd', picked, block_tiles, precision=lax.Precision...  60.8 us
  transfers between devices with their start and end apart: 73, of which 8 were waited for; matrix products, arithmetic and copies ran while one was open for 1% of the time, Pallas kernels for 0%

commit v1 on v0

v1 whole, which is shorter than its diff:
```python
import functools
import math

import jax
import jax.numpy as jnp
from jax import lax
from jax.experimental import pallas as pl
from jax.experimental.pallas import tpu as pltpu
from jax.sharding import PartitionSpec as P

DEG = 8
REACH = 12
B = 128
K = 24
R = 3
SPAN = R * 9
V = 32
GROUPS = 2
GV = V // GROUPS
W = R * B
MESH = pl.DeviceIdType.MESH
HIGH = lax.Precision.HIGHEST
F32 = jnp.float32
BF16 = jnp.bfloat16

ORDER = (0, 1, 2, -2, -1, 3, 4, -4, -3)
SLOT = {m: i for i, m in enumerate(ORDER)}
DIRECT = ((2, -2), (-2, 2), (4, -4), (-4, 4), (-3, -3), (1, 1))
FORWARD = ((2, -1), (-2, 3))
NSEND = len(DIRECT) + len(FORWARD)


def split(values):
    high = values.astype(BF16)
    low = (values - high.astype(F32)).astype(BF16)
    return high, low


def stacked(pieces):
    columns = []
    for piece in pieces:
        columns.append(jnp.concatenate(split(piece), axis=0))
    return jnp.concatenate(columns, axis=1)


def nt(a, b):
    return lax.dot_general(
        a, b, (((1,), (1,)), ((), ())), precision=HIGH, preferred_element_type=F32
    )


def nn(a, b):
    return jnp.dot(a, b, precision=HIGH, preferred_element_type=F32)


def kernel(
    order_total,
    tiles_hbm,
    pattern,
    start_hbm,
    center_ref,
    half_ref,
    pairs,
    out_ref,
    proj_ref,
    tiles,
    weights,
    inverse,
    held,
    halo,
    low,
    zbuf,
    xbuf,
    cbuf,
    tile_sem,
    start_sem,
    send_sem,
    recv_sem,
    low_send,
    low_recv,
    z_send,
    z_recv,
    x_send,
    x_recv,
    c_send,
    c_recv,
):
    me = lax.axis_index("row")
    cut = lax.axis_index("cuts")
    core = lax.rem(me, 2)
    chip = me // 2
    zpos = lax.rem(chip, 8)
    xpos = chip // 8
    sign = 1 - 2 * core

    def at(m):
        return {"row": lax.rem(me + m * sign + 64, 64)}

    def cut_at(step):
        return {"cuts": lax.rem(cut + step + 8, 8)}

    loads = []
    for g in range(GROUPS):
        load = pltpu.make_async_copy(
            start_hbm.at[0, pl.ds(g * GV, GV), :], held.at[g, 0], start_sem.at[g]
        )
        load.start()
        loads.append(load)
    tile_loads = []
    for i in range(R):
        load = pltpu.make_async_copy(tiles_hbm.at[i], tiles.at[i], tile_sem.at[i])
        load.start()
        tile_loads.append(load)

    barrier = pltpu.get_barrier_semaphore()
    for m in (-4, -3, -2, -1, 1, 2, 3, 4):
        pl.semaphore_signal(barrier, inc=1, device_id=at(m), device_id_type=MESH)
    for step in (-1, 1):
        pl.semaphore_signal(barrier, inc=1, device_id=cut_at(step), device_id_type=MESH)
    pl.semaphore_wait(barrier, 10)

    def remote(src, g, p, coordinate, target, index):
        return pltpu.make_async_remote_copy(
            src_ref=src,
            dst_ref=halo.at[g, p, SLOT[coordinate]],
            send_sem=send_sem.at[g, index],
            recv_sem=recv_sem.at[g, p, SLOT[coordinate]],
            device_id=at(target),
            device_id_type=MESH,
        )

    def direct(g, p, index):
        target, coordinate = DIRECT[index]
        return remote(held.at[g, p], g, p, coordinate, target, index)

    def forward(g, p, index):
        source, coordinate = FORWARD[index]
        return remote(
            halo.at[g, p, SLOT[source]], g, p, coordinate, 1, len(DIRECT) + index
        )

    def arrived(g, p, m):
        remote(held.at[g, p], g, p, m, 1, 0).wait_recv()

    def send(g, p):
        for index in range(len(DIRECT)):
            direct(g, p, index).start()

    for g in range(GROUPS):
        loads[g].wait()
        send(g, 0)
    for g in range(GROUPS):
        held[g, 1] = jnp.zeros((GV, W), F32)

    lowest = R * me - REACH

    def find(n, carry):
        i = n // SPAN
        t = n - i * SPAN
        column = lax.rem(lowest + t + 192, 192)
        found = jnp.int32(-1)
        for k in range(K):
            found = jnp.where(pattern[i, k] == column, k, found)
        inverse[n] = found
        return carry

    lax.fori_loop(0, R * SPAN, find, 0)

    for load in tile_loads:
        load.wait()

    for j, m in enumerate(ORDER):

        def build(b, carry, j=j, m=m):
            for i in range(R):
                t = R * m * sign + REACH + b
                index = inverse[i * SPAN + t]
                tile = tiles[i, jnp.maximum(index, 0)]
                tile = jnp.where(index >= 0, tile, 0.0)
                high, rest = split(tile.T)
                rows = pl.ds(pl.multiple_of(j * W + b * B, B), B)
                weights[rows, pl.ds(i * 2 * B, B)] = high
                weights[rows, pl.ds(i * 2 * B + B, B)] = rest
            return carry

        lax.fori_loop(0, R, build, 0)

    def product(g, p):
        def chunk(first, count):
            pieces = []
            for j in range(first, first + count):
                pieces.append(held[g, p] if j == 0 else halo[g, p, j])
            return jnp.dot(
                stacked(pieces),
                weights[pl.ds(first * W, count * W), :],
                preferred_element_type=F32,
            )

        for index, (source, _) in enumerate(FORWARD):
            arrived(g, p, source)
            forward(g, p, index).start()
        arrived(g, p, 1)
        total = chunk(0, 4)
        arrived(g, p, -1)
        arrived(g, p, 3)
        total += chunk(4, 2)
        arrived(g, p, 4)
        arrived(g, p, -4)
        arrived(g, p, -3)
        total += chunk(6, 3)
        columns = []
        for i in range(R):
            both = total[:, i * 2 * B : i * 2 * B + B] + total[:, i * 2 * B + B : (i + 1) * 2 * B]
            columns.append(both[:GV] + both[GV:])
        return jnp.concatenate(columns, axis=1)

    def sent(g, p):
        for index in range(len(DIRECT)):
            direct(g, p, index).wait_send()
        for index in range(len(FORWARD)):
            forward(g, p, index).wait_send()

    center = center_ref[0]
    inverse_half = 1.0 / jnp.full((GV, W), half_ref[0], F32)

    def steps(n, carry):
        for p in (0, 1):
            factor = jnp.where(n * 2 + p == 0, 1.0, 2.0).astype(F32)
            for g in range(GROUPS):
                applied = product(g, p)
                following = (
                    factor * (applied - center * held[g, p]) * inverse_half - held[g, 1 - p]
                )
                sent(g, p)
                held[g, 1 - p] = following
                send(g, 1 - p)
        return carry

    lax.fori_loop(0, DEG // 2, steps, 0)

    def to_next(g):
        return pltpu.make_async_remote_copy(
            src_ref=held.at[g, 0],
            dst_ref=low.at[g],
            send_sem=low_send.at[g],
            recv_sem=low_recv.at[g],
            device_id=cut_at(1),
            device_id_type=MESH,
        )

    for g in range(GROUPS):
        to_next(g).start()
    imaged = []
    for g in range(GROUPS):
        imaged.append(product(g, 0))
        sent(g, 0)
    imaged = jnp.concatenate(imaged, axis=0)
    for g in range(GROUPS):
        to_next(g).wait()
    current = jnp.concatenate([held[g, 0] for g in range(GROUPS)], axis=0)
    lower = jnp.concatenate([low[g] for g in range(GROUPS)], axis=0)
    none = jnp.zeros((V, W), F32)
    partial = nt(current, jnp.concatenate([current, lower, imaged, none], axis=0)) + nt(
        lower, jnp.concatenate([none, none, none, lower], axis=0)
    )

    def gather(value, buffer, count, own, send_sems, recv_sems, device):
        buffer[own] = value
        copies = []
        for step in range(1, count):
            there = lax.rem(own + step, count)
            copy = pltpu.make_async_remote_copy(
                src_ref=buffer.at[own],
                dst_ref=buffer.at[own],
                send_sem=send_sems.at[step],
                recv_sem=recv_sems.at[step],
                device_id={"row": device(there)},
                device_id_type=MESH,
            )
            copy.start()
            copies.append(copy)
        for copy in copies:
            copy.wait()
        total = buffer[0]
        for n in range(1, count):
            total = total + buffer[n]
        return total

    total = gather(partial, zbuf, 8, zpos, z_send, z_recv, lambda z: (xpos * 8 + z) * 2 + core)
    total = gather(total, xbuf, 4, xpos, x_send, x_recv, lambda x: (x * 8 + zpos) * 2 + core)
    total = gather(total, cbuf, 2, core, c_send, c_recv, lambda k: chip * 2 + k)

    lane = lax.broadcasted_iota(jnp.int32, (V, 4 * V), 1)
    row = lax.broadcasted_iota(jnp.int32, (V, 4 * V), 0)
    unit = jnp.where((lane == row + V) | (lane == row + 2 * V), 1.0, 0.0).astype(F32)
    inner = (lane >= V) & (lane < 3 * V)
    left = lane < 2 * V
    table = jnp.where(inner, unit, total)
    for j in range(V - 1):
        pivot_row = table[j : j + 1, :]
        column = jnp.where(left, table[:, j : j + 1], table[:, 3 * V + j : 3 * V + j + 1])
        pivot = jnp.where(
            left[:1], pivot_row[:, j : j + 1], pivot_row[:, 3 * V + j : 3 * V + j + 1]
        )
        scaled = pivot_row / pivot
        table = table - jnp.where(row > j, column * scaled, 0.0)
    diagonal_left = jnp.sum(jnp.where(lane == row, table, 0.0), axis=1, keepdims=True)
    diagonal_right = jnp.sum(jnp.where(lane == row + 3 * V, table, 0.0), axis=1, keepdims=True)
    table = table / jnp.sqrt(jnp.where(left, diagonal_left, diagonal_right))
    table = jnp.where(inner, table, 0.0)
    factor_inverse = pltpu.roll(table, 3 * V, 1)[:, :V]
    lower_inverse = pltpu.roll(table, 2 * V, 1)[:, :V]
    half_way = nn(factor_inverse, total)
    cross = nt(pltpu.roll(half_way, 3 * V, 1)[:, :V], lower_inverse)
    proj_ref[0] = nt(pltpu.roll(half_way, 2 * V, 1)[:, :V], factor_inverse)
    small_row = lax.broadcasted_iota(jnp.int32, (V, V), 0)
    small_lane = lax.broadcasted_iota(jnp.int32, (V, V), 1)
    chosen = jnp.zeros((V, V), F32)
    for p in range(8):
        chosen += jnp.where(
            (small_row == pairs[0, p, 0]) & (small_lane == pairs[0, p, 1]), 1.0, 0.0
        )
    removed = nn(chosen * cross, table)
    removed = jnp.where(cut > 0, removed, 0.0)
    mixing = jnp.where(left, table, -removed)
    lower = jnp.where(cut > 0, lower, 0.0)
    out_ref[0] = math.sqrt(order_total) * nn(
        mixing, jnp.concatenate([none, current, lower, none], axis=0)
    )


def local(block_tiles, tile_pattern, start_vectors, centers, halfwidths, dup_pairs):
    order_total = start_vectors.shape[2] * lax.axis_size("row")
    smem = pl.BlockSpec(memory_space=pltpu.SMEM)
    vmem = pl.BlockSpec(memory_space=pltpu.VMEM)
    anywhere = pl.BlockSpec(memory_space=pl.ANY)
    dma = pltpu.SemaphoreType.DMA
    return pl.pallas_call(
        functools.partial(kernel, order_total),
        out_shape=(
            jax.ShapeDtypeStruct((1, V, W), F32),
            jax.ShapeDtypeStruct((1, V, V), F32),
        ),
        in_specs=[anywhere, smem, anywhere, smem, smem, smem],
        out_specs=(vmem, vmem),
        scratch_shapes=[
            pltpu.VMEM((R, K, B, B), F32),
            pltpu.VMEM((9 * W, 2 * W), BF16),
            pltpu.SMEM((R * SPAN,), jnp.int32),
            pltpu.VMEM((GROUPS, 2, GV, W), F32),
            pltpu.VMEM((GROUPS, 2, 9, GV, W), F32),
            pltpu.VMEM((GROUPS, GV, W), F32),
            pltpu.VMEM((8, V, 4 * V), F32),
            pltpu.VMEM((4, V, 4 * V), F32),
            pltpu.VMEM((2, V, 4 * V), F32),
            dma((R,)),
            dma((GROUPS,)),
            dma((GROUPS, NSEND)),
            dma((GROUPS, 2, 9)),
            dma((GROUPS,)),
            dma((GROUPS,)),
            dma((8,)),
            dma((8,)),
            dma((4,)),
            dma((4,)),
            dma((2,)),
            dma((2,)),
        ],
        compiler_params=pltpu.CompilerParams(
            collective_id=0, has_side_effects=True, vmem_limit_bytes=48 << 20
        ),
    )(block_tiles, tile_pattern, start_vectors, centers, halfwidths, dup_pairs)


def solution(mesh):
    in_specs = (
        P("row", None, None, None),
        P("row", None),
        P("cuts", None, "row"),
        P("cuts"),
        P("cuts"),
        P("cuts", None, None),
    )
    out_specs = (P("cuts", None, "row"), P("cuts", None, None))
    return jax.shard_map(local, mesh=mesh, in_specs=in_specs, out_specs=out_specs, check_vma=False)
```

time: 864 us -> 107 us (0.12)
  blocking collectives: 491 us -> 0 us
  starting transfers between devices: 269 us -> 0 us
  Pallas kernels: 0 us -> 97 us
  matrix products: 62.8 us -> 0 us
  waiting for transfers between devices: 15.6 us -> 0 us
    psum x2 -> x0, blocking collectives: 491 us -> none  [the longest x1 246 us: local(): lax.psum(jnp.dot(current, current.T, precision=lax.Precision.HIGHEST), 'r...]
    ppermute x73 -> x0, starting transfers between devices: 269 us -> none  [the longest x72 266 us: from_behind(): lax.ppermute(shard, axis, [(i, (i + by) % size) for i in range(size)])]
    pallas_call x0 -> x1, Pallas kernels: none -> 97 us  [local(): pl.pallas_call(functools.partial(kernel, order_total), out_shape=(jax.Sha...]
    dot_general x14 -> x0, matrix products: 62.5 us -> none  [the longest x9 60.8 us: apply_local(): jnp.einsum('vrkc,rkdc->vrd', picked, block_tiles, precision=lax.Precision...]
    ppermute x73 -> x0, waiting for transfers between devices: 15.6 us -> none  [the longest x72 15.6 us: from_behind(): lax.ppermute(shard, axis, [(i, (i + by) % size) for i in range(size)])]
  transfers between devices with their start and end apart: 73 -> 0, of which waited for: 8 -> 0; matrix products, arithmetic and copies ran while one was open for 1% -> 0% of each run, Pallas kernels for 0% -> 0%
where the time goes in v1:
time: 107 us; the launch traced here: 105 us
  Pallas kernels  97 us (91%)
  local copies, waits for them, and re-layouts  5.8 us (5%)
  between operations  1.93 us (2%)
    pallas_call x1, Pallas kernels, local(): pl.pallas_call(functools.partial(kernel, order_total), out_shape=(jax.Sha...  97 us
    unnamed x9, local copies, waits for them, and re-layouts  5.8 us

profile of v1, /device:TPU:1, one launch (start us, length us, event | category | flops | bytes accessed | tf_op | source)
XLA Modules:
  0.0 104.7 jit_solution(13304151086730271942)
XLA Ops:
  1.9 0.8 copy.8.pairs
  2.7 0.0 copy-start
  2.7 2.3 %copy-done = f32[3,24,128,128]{3,2,1,0:T(8,128)S(1)} copy-done((f32[3,24,128,128]{3,2,1,0:T(8,128)S(1)}, f32[3,24,128,128]{3,2,1,0:T(8,128)}, u32[]{:S(2)}) %copy-start) | copy-done | bytes 4718616
  5.0 0.0 copy-start.1
  5.0 0.8 copy-done.1
  5.8 0.0 copy-start.2
  5.8 0.7 copy-done.2
  6.5 97.0 %shard_map.77 = (f32[1,32,384]{2,1,0:T(8,128)S(1)}, f32[1,32,32]{2,1,0:T(8,128)S(1)}) custom-call(f32[3,24,128,128]{3,2,1,0:T(8,128)S(1)} %copy-done, s32[3,24]{1,0:T(4,128)S(1)} %copy-done.2, f32[1,32,384]{2,1,0:T(8,128)S(1)} %copy-done.1, f32[1]{0:T(128)S(6)} %copy.11.center_ref, f32[1]{0:T(128)S(6)} %copy.12.half_ref, s32[1,8,2]{2,1,0:T(8,128)S(1)} %copy.8.pairs), custom_call_target="tpu_custom_call" | custom-call | tf_op jit(solution)/shard_map/pallas_call | solution.py:338
  103.5 0.6 copy.13
  104.1 0.6 copy.14
Async XLA Ops:
  2.7 2.3 %copy-start = (f32[3,24,128,128]{3,2,1,0:T(8,128)S(1)}, f32[3,24,128,128]{3,2,1,0:T(8,128)}, u32[]{:S(2)}) copy-start(f32[3,24,128,128]{3,2,1,0:T(8,128)} %tiles_hbm.1) | copy-start | bytes 14155780
  5.0 0.8 copy-start.1
  5.8 0.7 copy-start.2

commit v2 on v1

--- a/solution.py
+++ b/solution.py
@@ -56,13 +56,17 @@
 def kernel(
     order_total,
     tiles_hbm,
+    pattern_hbm,
+    start_hbm,
+    center_hbm,
+    half_hbm,
+    pairs_hbm,
+    out_ref,
+    proj_ref,
     pattern,
-    start_hbm,
     center_ref,
     half_ref,
     pairs,
-    out_ref,
-    proj_ref,
     tiles,
     weights,
     inverse,
@@ -84,6 +88,9 @@
     x_recv,
     c_send,
     c_recv,
+    factor_buf,
+    factor_sem,
+    small_sem,
 ):
     me = lax.axis_index("row")
     cut = lax.axis_index("cuts")
@@ -99,6 +106,18 @@
     def cut_at(step):
         return {"cuts": lax.rem(cut + step + 8, 8)}
 
+    small_loads = []
+    for n, (source, target) in enumerate(
+        (
+            (pattern_hbm, pattern),
+            (center_hbm, center_ref),
+            (half_hbm, half_ref),
+            (pairs_hbm, pairs),
+        )
+    ):
+        load = pltpu.make_async_copy(source, target, small_sem.at[n])
+        load.start()
+        small_loads.append(load)
     loads = []
     for g in range(GROUPS):
         load = pltpu.make_async_copy(
@@ -151,6 +170,9 @@
         send(g, 0)
     for g in range(GROUPS):
         held[g, 1] = jnp.zeros((GV, W), F32)
+
+    for load in small_loads:
+        load.wait()
 
     lowest = R * me - REACH
 
@@ -169,21 +191,22 @@
     for load in tile_loads:
         load.wait()
 
-    for j, m in enumerate(ORDER):
-
-        def build(b, carry, j=j, m=m):
+    def build(j, carry):
+        m = jnp.int32(0)
+        for slot, source in enumerate(ORDER):
+            m = jnp.where(j == slot, source, m)
+        for b in range(R):
+            rows = pl.ds(pl.multiple_of(j * W + b * B, B), B)
             for i in range(R):
-                t = R * m * sign + REACH + b
-                index = inverse[i * SPAN + t]
+                index = inverse[i * SPAN + R * m * sign + REACH + b]
                 tile = tiles[i, jnp.maximum(index, 0)]
                 tile = jnp.where(index >= 0, tile, 0.0)
                 high, rest = split(tile.T)
-                rows = pl.ds(pl.multiple_of(j * W + b * B, B), B)
                 weights[rows, pl.ds(i * 2 * B, B)] = high
                 weights[rows, pl.ds(i * 2 * B + B, B)] = rest
-            return carry
-
-        lax.fori_loop(0, R, build, 0)
+        return carry
+
+    lax.fori_loop(0, len(ORDER), build, 0)
 
     def product(g, p):
         def chunk(first, count):
@@ -196,9 +219,6 @@
                 preferred_element_type=F32,
             )
 
-        for index, (source, _) in enumerate(FORWARD):
-            arrived(g, p, source)
-            forward(g, p, index).start()
         arrived(g, p, 1)
         total = chunk(0, 4)
         arrived(g, p, -1)
@@ -214,6 +234,11 @@
             columns.append(both[:GV] + both[GV:])
         return jnp.concatenate(columns, axis=1)
 
+    def pass_on(g, p):
+        for index, (source, _) in enumerate(FORWARD):
+            arrived(g, p, source)
+            forward(g, p, index).start()
+
     def sent(g, p):
         for index in range(len(DIRECT)):
             direct(g, p, index).wait_send()
@@ -227,6 +252,7 @@
         for p in (0, 1):
             factor = jnp.where(n * 2 + p == 0, 1.0, 2.0).astype(F32)
             for g in range(GROUPS):
+                pass_on(g, p)
                 applied = product(g, p)
                 following = (
                     factor * (applied - center * held[g, p]) * inverse_half - held[g, 1 - p]
@@ -250,90 +276,127 @@
 
     for g in range(GROUPS):
         to_next(g).start()
-    imaged = []
-    for g in range(GROUPS):
-        imaged.append(product(g, 0))
-        sent(g, 0)
-    imaged = jnp.concatenate(imaged, axis=0)
-    for g in range(GROUPS):
-        to_next(g).wait()
     current = jnp.concatenate([held[g, 0] for g in range(GROUPS)], axis=0)
-    lower = jnp.concatenate([low[g] for g in range(GROUPS)], axis=0)
-    none = jnp.zeros((V, W), F32)
-    partial = nt(current, jnp.concatenate([current, lower, imaged, none], axis=0)) + nt(
-        lower, jnp.concatenate([none, none, none, lower], axis=0)
-    )
-
-    def gather(value, buffer, count, own, send_sems, recv_sems, device):
-        buffer[own] = value
-        copies = []
+
+    def narrow(left, right):
+        none = jnp.zeros((3 * V, W), F32)
+        value = nt(left, jnp.concatenate([right, none], axis=0))
+        return packed(value)
+
+    def packed(value):
+        total = value[:8]
+        for q in range(1, 4):
+            total = total + pltpu.roll(value[8 * q : 8 * q + 8], V * q, 1)
+        return total
+
+    def unpacked(value):
+        parts = [value] + [pltpu.roll(value, 4 * V - V * q, 1) for q in range(1, 4)]
+        return jnp.concatenate(parts, axis=0)
+
+    def copies(a, phase):
+        buffer, send_sems, recv_sems, own, device = phase
+        count = buffer.shape[1]
+        result = []
         for step in range(1, count):
             there = lax.rem(own + step, count)
-            copy = pltpu.make_async_remote_copy(
-                src_ref=buffer.at[own],
-                dst_ref=buffer.at[own],
-                send_sem=send_sems.at[step],
-                recv_sem=recv_sems.at[step],
-                device_id={"row": device(there)},
-                device_id_type=MESH,
+            result.append(
+                pltpu.make_async_remote_copy(
+                    src_ref=buffer.at[a, own],
+                    dst_ref=buffer.at[a, own],
+                    send_sem=send_sems.at[a, step],
+                    recv_sem=recv_sems.at[a, step],
+                    device_id={"row": device(there)},
+                    device_id_type=MESH,
+                )
             )
+        return result
+
+    def begin(a, phase, value):
+        phase[0][a, phase[3]] = value
+        for copy in copies(a, phase):
             copy.start()
-            copies.append(copy)
-        for copy in copies:
+
+    def finish(a, phase):
+        for copy in copies(a, phase):
             copy.wait()
-        total = buffer[0]
-        for n in range(1, count):
-            total = total + buffer[n]
+        total = phase[0][a, 0]
+        for n in range(1, phase[0].shape[1]):
+            total = total + phase[0][a, n]
         return total
 
-    total = gather(partial, zbuf, 8, zpos, z_send, z_recv, lambda z: (xpos * 8 + z) * 2 + core)
-    total = gather(total, xbuf, 4, xpos, x_send, x_recv, lambda x: (x * 8 + zpos) * 2 + core)
-    total = gather(total, cbuf, 2, core, c_send, c_recv, lambda k: chip * 2 + k)
+    along_z = (zbuf, z_send, z_recv, zpos, lambda z: (xpos * 8 + z) * 2 + core)
+    along_x = (xbuf, x_send, x_recv, xpos, lambda x: (x * 8 + zpos) * 2 + core)
+    in_chip = (cbuf, c_send, c_recv, core, lambda k: chip * 2 + k)
+
+    GRAM, CROSS, QUOTIENT = 0, 1, 2
+    begin(GRAM, along_z, narrow(current, current))
+    pass_on(0, 0)
+    imaged = [product(0, 0)]
+    pass_on(1, 0)
+    for g in range(GROUPS):
+        to_next(g).wait()
+    lower = jnp.concatenate([low[g] for g in range(GROUPS)], axis=0)
+    begin(CROSS, along_z, narrow(current, lower))
+    begin(GRAM, along_x, finish(GRAM, along_z))
+    imaged.append(product(1, 0))
+    begin(QUOTIENT, along_z, narrow(current, jnp.concatenate(imaged, axis=0)))
+    for g in range(GROUPS):
+        sent(g, 0)
+    begin(CROSS, along_x, finish(CROSS, along_z))
+    begin(GRAM, in_chip, finish(GRAM, along_x))
+    gram = unpacked(finish(GRAM, in_chip))
 
     lane = lax.broadcasted_iota(jnp.int32, (V, 4 * V), 1)
     row = lax.broadcasted_iota(jnp.int32, (V, 4 * V), 0)
-    unit = jnp.where((lane == row + V) | (lane == row + 2 * V), 1.0, 0.0).astype(F32)
-    inner = (lane >= V) & (lane < 3 * V)
-    left = lane < 2 * V
-    table = jnp.where(inner, unit, total)
-    for j in range(V - 1):
-        pivot_row = table[j : j + 1, :]
-        column = jnp.where(left, table[:, j : j + 1], table[:, 3 * V + j : 3 * V + j + 1])
-        pivot = jnp.where(
-            left[:1], pivot_row[:, j : j + 1], pivot_row[:, 3 * V + j : 3 * V + j + 1]
-        )
-        scaled = pivot_row / pivot
-        table = table - jnp.where(row > j, column * scaled, 0.0)
-    diagonal_left = jnp.sum(jnp.where(lane == row, table, 0.0), axis=1, keepdims=True)
-    diagonal_right = jnp.sum(jnp.where(lane == row + 3 * V, table, 0.0), axis=1, keepdims=True)
-    table = table / jnp.sqrt(jnp.where(left, diagonal_left, diagonal_right))
-    table = jnp.where(inner, table, 0.0)
-    factor_inverse = pltpu.roll(table, 3 * V, 1)[:, :V]
-    lower_inverse = pltpu.roll(table, 2 * V, 1)[:, :V]
-    half_way = nn(factor_inverse, total)
-    cross = nt(pltpu.roll(half_way, 3 * V, 1)[:, :V], lower_inverse)
-    proj_ref[0] = nt(pltpu.roll(half_way, 2 * V, 1)[:, :V], factor_inverse)
+    table = jnp.where(lane < V, gram, jnp.where(lane == row + V, 1.0, 0.0))
+
+    def eliminate(table, first, last):
+        for j in range(first, last):
+            scaled = table[j : j + 1, :] / table[j : j + 1, j : j + 1]
+            table = table - jnp.where(row > j, table[:, j : j + 1] * scaled, 0.0)
+        return table
+
+    table = eliminate(table, 0, V // 2)
+    begin(QUOTIENT, along_x, finish(QUOTIENT, along_z))
+    table = eliminate(table, V // 2, V - 1)
+    diagonal = jnp.sum(jnp.where(lane == row, table, 0.0), axis=1, keepdims=True)
+    table = jnp.where(lane < V, 0.0, table) / jnp.sqrt(diagonal)
+    table = pltpu.roll(table, 3 * V, 1)
+    factor_buf[0] = packed(table)
+    factor_copy = pltpu.make_async_remote_copy(
+        src_ref=factor_buf.at[0],
+        dst_ref=factor_buf.at[1],
+        send_sem=factor_sem.at[0],
+        recv_sem=factor_sem.at[1],
+        device_id=cut_at(1),
+        device_id_type=MESH,
+    )
+    factor_copy.start()
+    factor_inverse = table[:, :V]
+    begin(CROSS, in_chip, finish(CROSS, along_x))
+    basis = nn(factor_inverse, current)
     small_row = lax.broadcasted_iota(jnp.int32, (V, V), 0)
     small_lane = lax.broadcasted_iota(jnp.int32, (V, V), 1)
     chosen = jnp.zeros((V, V), F32)
     for p in range(8):
         chosen += jnp.where(
-            (small_row == pairs[0, p, 0]) & (small_lane == pairs[0, p, 1]), 1.0, 0.0
-        )
-    removed = nn(chosen * cross, table)
-    removed = jnp.where(cut > 0, removed, 0.0)
-    mixing = jnp.where(left, table, -removed)
-    lower = jnp.where(cut > 0, lower, 0.0)
-    out_ref[0] = math.sqrt(order_total) * nn(
-        mixing, jnp.concatenate([none, current, lower, none], axis=0)
-    )
+            (small_row == pairs[0, 0, p]) & (small_lane == pairs[0, 1, p]), 1.0, 0.0
+        )
+    begin(QUOTIENT, in_chip, finish(QUOTIENT, along_x))
+    cross = nn(factor_inverse, unpacked(finish(CROSS, in_chip))[:, :V])
+    factor_copy.wait()
+    lower_inverse = unpacked(factor_buf[1])[:, :V]
+    lower_basis = jnp.where(cut > 0, nn(lower_inverse, lower), 0.0)
+    removed = jnp.where(cut > 0, chosen * nt(cross, lower_inverse), 0.0)
+    out_ref[0] = math.sqrt(order_total) * (basis - nn(removed, lower_basis))
+    quotient = unpacked(finish(QUOTIENT, in_chip))[:, :V]
+    proj_ref[0] = nt(nn(factor_inverse, quotient), factor_inverse)
 
 
 def local(block_tiles, tile_pattern, start_vectors, centers, halfwidths, dup_pairs):
     order_total = start_vectors.shape[2] * lax.axis_size("row")
-    smem = pl.BlockSpec(memory_space=pltpu.SMEM)
     vmem = pl.BlockSpec(memory_space=pltpu.VMEM)
-    anywhere = pl.BlockSpec(memory_space=pl.ANY)
+    hbm = pl.BlockSpec(memory_space=pltpu.HBM)
     dma = pltpu.SemaphoreType.DMA
     return pl.pallas_call(
         functools.partial(kernel, order_total),
@@ -341,35 +404,49 @@
             jax.ShapeDtypeStruct((1, V, W), F32),
             jax.ShapeDtypeStruct((1, V, V), F32),
         ),
-        in_specs=[anywhere, smem, anywhere, smem, smem, smem],
+        in_specs=[hbm] * 6,
         out_specs=(vmem, vmem),
         scratch_shapes=[
+            pltpu.SMEM((R, K), jnp.int32),
+            pltpu.SMEM((1,), F32),
+            pltpu.SMEM((1,), F32),
+            pltpu.SMEM((1, 2, 8), jnp.int32),
             pltpu.VMEM((R, K, B, B), F32),
             pltpu.VMEM((9 * W, 2 * W), BF16),
             pltpu.SMEM((R * SPAN,), jnp.int32),
             pltpu.VMEM((GROUPS, 2, GV, W), F32),
             pltpu.VMEM((GROUPS, 2, 9, GV, W), F32),
             pltpu.VMEM((GROUPS, GV, W), F32),
-            pltpu.VMEM((8, V, 4 * V), F32),
-            pltpu.VMEM((4, V, 4 * V), F32),
-            pltpu.VMEM((2, V, 4 * V), F32),
+            pltpu.VMEM((3, 8, 8, 4 * V), F32),
+            pltpu.VMEM((3, 4, 8, 4 * V), F32),
+            pltpu.VMEM((3, 2, 8, 4 * V), F32),
             dma((R,)),
             dma((GROUPS,)),
             dma((GROUPS, NSEND)),
             dma((GROUPS, 2, 9)),
             dma((GROUPS,)),
             dma((GROUPS,)),
-            dma((8,)),
-            dma((8,)),
+            dma((3, 8)),
+            dma((3, 8)),
+            dma((3, 4)),
+            dma((3, 4)),
+            dma((3, 2)),
+            dma((3, 2)),
+            pltpu.VMEM((2, 8, 4 * V), F32),
+            dma((2,)),
             dma((4,)),
-            dma((4,)),
-            dma((2,)),
-            dma((2,)),
         ],
         compiler_params=pltpu.CompilerParams(
-            collective_id=0, has_side_effects=True, vmem_limit_bytes=48 << 20
+            collective_id=0, has_side_effects=True, vmem_limit_bytes=60 << 20
         ),
-    )(block_tiles, tile_pattern, start_vectors, centers, halfwidths, dup_pairs)
+    )(
+        block_tiles,
+        tile_pattern,
+        start_vectors,
+        centers,
+        halfwidths,
+        jnp.transpose(dup_pairs, (0, 2, 1)),
+    )
 
 
 def solution(mesh):

time: 107 us -> 99.3 us (0.928); the launches traced: 105 us -> 99 us
  local copies, waits for them, and re-layouts: 5.8 us -> 2.74 us
  Pallas kernels: 97 us -> 94.4 us
    unnamed x9 -> x2, local copies, waits for them, and re-layouts: 5.8 us -> 2.74 us
    pallas_call x1, Pallas kernels: 97 us -> 94.4 us  [local(): pl.pallas_call(functools.partial(kernel, order_total), out_shape=(jax.Sha...]
where the time goes in v2:
time: 99.3 us; the launch traced here: 99 us
  Pallas kernels  94.4 us (95%)
  local copies, waits for them, and re-layouts  2.74 us (3%)
  between operations  1.93 us (2%)
    pallas_call x1, Pallas kernels, local(): pl.pallas_call(functools.partial(kernel, order_total), out_shape=(jax.Sha...  94.4 us
    unnamed x2, local copies, waits for them, and re-layouts  2.74 us

profile of v2, /device:TPU:1, one launch (start us, length us, event | category | flops | bytes accessed | tf_op | source)
XLA Modules:
  0.0 99.0 jit_solution(1466034964777149558)
XLA Ops:
  1.9 94.4 %shard_map.77 = (f32[1,32,384]{2,1,0:T(8,128)}, f32[1,32,32]{2,1,0:T(8,128)}) custom-call(f32[3,24,128,128]{3,2,1,0:T(8,128)} %tiles_hbm.1, s32[3,24]{1,0:T(4,128)} %pattern_hbm.1, f32[1,32,384]{2,1,0:T(8,128)} %start_hbm.1, f32[1]{0:T(128)S(6)} %copy.10.center_hbm, f32[1]{0:T(128)S(6)} %copy.11.half_hbm, s32[1,2,8]{2,1,0:T(2,128)} %bitcast.1), custom_call_target="tpu_custom_call" | custom-call | tf_op jit(solution)/shard_map/pallas_call | solution.py:401
  96.3 1.4 %copy.12 = f32[1,32,384]{2,1,0:T(8,128)} copy(f32[1,32,384]{2,1,0:T(8,128)} %get-tuple-element.4) | data formatting | bytes 98304
  97.7 1.3 %copy.13 = f32[1,32,32]{2,1,0:T(8,128)} copy(f32[1,32,32]{2,1,0:T(8,128)} %get-tuple-element.5) | data formatting | bytes 8192

commit v3 on v2

--- a/solution.py
+++ b/solution.py
@@ -23,7 +23,7 @@
 F32 = jnp.float32
 BF16 = jnp.bfloat16
 
-ORDER = (0, 1, 2, -2, -1, 3, 4, -4, -3)
+ORDER = (0, 1, 2, -2, -1, 3, -4, 4, -3)
 SLOT = {m: i for i, m in enumerate(ORDER)}
 DIRECT = ((2, -2), (-2, 2), (4, -4), (-4, 4), (-3, -3), (1, 1))
 FORWARD = ((2, -1), (-2, 3))
@@ -223,11 +223,11 @@
         total = chunk(0, 4)
         arrived(g, p, -1)
         arrived(g, p, 3)
-        total += chunk(4, 2)
+        arrived(g, p, -4)
+        total += chunk(4, 3)
         arrived(g, p, 4)
-        arrived(g, p, -4)
         arrived(g, p, -3)
-        total += chunk(6, 3)
+        total += chunk(7, 2)
         columns = []
         for i in range(R):
             both = total[:, i * 2 * B : i * 2 * B + B] + total[:, i * 2 * B + B : (i + 1) * 2 * B]
@@ -393,17 +393,30 @@
     proj_ref[0] = nt(nn(factor_inverse, quotient), factor_inverse)
 
 
+def write(filtered, quotient, out_ref, proj_ref, sem):
+    copies = [
+        pltpu.make_async_copy(filtered, out_ref, sem.at[0]),
+        pltpu.make_async_copy(quotient, proj_ref, sem.at[1]),
+    ]
+    for copy in copies:
+        copy.start()
+    for copy in copies:
+        copy.wait()
+
+
 def local(block_tiles, tile_pattern, start_vectors, centers, halfwidths, dup_pairs):
     order_total = start_vectors.shape[2] * lax.axis_size("row")
     vmem = pl.BlockSpec(memory_space=pltpu.VMEM)
     hbm = pl.BlockSpec(memory_space=pltpu.HBM)
     dma = pltpu.SemaphoreType.DMA
-    return pl.pallas_call(
+    fixed = lambda operand: pltpu.with_memory_space_constraint(operand, pltpu.HBM)
+    shapes = (
+        jax.ShapeDtypeStruct((1, V, W), F32),
+        jax.ShapeDtypeStruct((1, V, V), F32),
+    )
+    results = pl.pallas_call(
         functools.partial(kernel, order_total),
-        out_shape=(
-            jax.ShapeDtypeStruct((1, V, W), F32),
-            jax.ShapeDtypeStruct((1, V, V), F32),
-        ),
+        out_shape=shapes,
         in_specs=[hbm] * 6,
         out_specs=(vmem, vmem),
         scratch_shapes=[
@@ -437,16 +450,24 @@
             dma((4,)),
         ],
         compiler_params=pltpu.CompilerParams(
-            collective_id=0, has_side_effects=True, vmem_limit_bytes=60 << 20
+            collective_id=0, has_side_effects=True, vmem_limit_bytes=52 << 20
         ),
     )(
-        block_tiles,
-        tile_pattern,
-        start_vectors,
+        fixed(block_tiles),
+        fixed(tile_pattern),
+        fixed(start_vectors),
         centers,
         halfwidths,
-        jnp.transpose(dup_pairs, (0, 2, 1)),
+        fixed(jnp.transpose(dup_pairs, (0, 2, 1))),
     )
+    return pl.pallas_call(
+        write,
+        out_shape=shapes,
+        in_specs=[pl.BlockSpec(memory_space=pl.ANY)] * 2,
+        out_specs=(hbm, hbm),
+        scratch_shapes=[dma((2,))],
+        compiler_params=pltpu.CompilerParams(vmem_limit_bytes=1 << 20),
+    )(*results)
 
 
 def solution(mesh):

time: 99.3 us -> 95.3 us (0.960)
  local copies, waits for them, and re-layouts: 2.74 us -> 0 us
  Pallas kernels: 94.4 us -> 93.2 us
    unnamed x2 -> x0, local copies, waits for them, and re-layouts: 2.74 us -> none
    pallas_call x1 -> x2, Pallas kernels: 94.4 us -> 93.2 us  [the longest x1 92.6 us: local(): pl.pallas_call(functools.partial(kernel, order_total), out_shape=shapes,...]
where the time goes in v3:
time: 95.3 us; the launch traced here: 95.1 us
  Pallas kernels  93.2 us (98%)
  between operations  1.93 us (2%)
    pallas_call x1, Pallas kernels, local(): pl.pallas_call(functools.partial(kernel, order_total), out_shape=shapes,...  92.6 us

profile of v3, /device:TPU:1, one launch (start us, length us, event | category | flops | bytes accessed | tf_op | source)
XLA Modules:
  0.0 95.1 jit_solution(10234103172407897704)
XLA Ops:
  1.9 92.6 %shard_map.77 = (f32[1,32,384]{2,1,0:T(8,128)S(1)}, f32[1,32,32]{2,1,0:T(8,128)S(1)}) custom-call(f32[3,24,128,128]{3,2,1,0:T(8,128)} %tiles_hbm.1, s32[3,24]{1,0:T(4,128)} %pattern_hbm.1, f32[1,32,384]{2,1,0:T(8,128)} %start_hbm.1, f32[1]{0:T(128)S(6)} %copy.8.center_hbm, f32[1]{0:T(128)S(6)} %copy.9.half_hbm, s32[1,2,8]{2,1,0:T(2,128)} %bitcast.1), custom_call_target="tpu_custom_call" | custom-call | tf_op jit(solution)/shard_map/pallas_call | solution.py:417
  94.5 0.6 shard_map.78

commit v4 on v3

--- a/solution.py
+++ b/solution.py
@@ -25,8 +25,8 @@
 
 ORDER = (0, 1, 2, -2, -1, 3, -4, 4, -3)
 SLOT = {m: i for i, m in enumerate(ORDER)}
-DIRECT = ((2, -2), (-2, 2), (4, -4), (-4, 4), (-3, -3), (1, 1))
-FORWARD = ((2, -1), (-2, 3))
+DIRECT = ((2, -2), (-2, 2), (-1, -1), (3, 3), (4, -4), (-4, 4), (-3, -3), (1, 1))
+FORWARD = ()
 NSEND = len(DIRECT) + len(FORWARD)
 
 
@@ -220,6 +220,8 @@
             )
 
         arrived(g, p, 1)
+        arrived(g, p, 2)
+        arrived(g, p, -2)
         total = chunk(0, 4)
         arrived(g, p, -1)
         arrived(g, p, 3)

time: 95.3 us -> 99.2 us (1.041)
  Pallas kernels: 93.2 us -> 96.5 us
    pallas_call x1, Pallas kernels: 92.6 us -> 95.8 us  [local(): pl.pallas_call(functools.partial(kernel, order_total), out_shape=shapes,...]
where the time goes in v4:
time: 99.2 us; the launch traced here: 98.4 us
  Pallas kernels  96.5 us (97%)
  between operations  1.93 us (2%)
    pallas_call x1, Pallas kernels, local(): pl.pallas_call(functools.partial(kernel, order_total), out_shape=shapes,...  95.8 us

profile of v4, /device:TPU:1, one launch (start us, length us, event | category | flops | bytes accessed | tf_op | source)
XLA Modules:
  0.0 98.4 jit_solution(660996840911469180)
XLA Ops:
  1.9 95.8 %shard_map.77 = (f32[1,32,384]{2,1,0:T(8,128)S(1)}, f32[1,32,32]{2,1,0:T(8,128)S(1)}) custom-call(f32[3,24,128,128]{3,2,1,0:T(8,128)} %tiles_hbm.1, s32[3,24]{1,0:T(4,128)} %pattern_hbm.1, f32[1,32,384]{2,1,0:T(8,128)} %start_hbm.1, f32[1]{0:T(128)S(6)} %copy.8.center_hbm, f32[1]{0:T(128)S(6)} %copy.9.half_hbm, s32[1,2,8]{2,1,0:T(2,128)} %bitcast.1), custom_call_target="tpu_custom_call" | custom-call | tf_op jit(solution)/shard_map/pallas_call | solution.py:419
  97.8 0.6 shard_map.78
